TPU v7x, 32 devices: a whole 2x2x4 slice. The times are simulated.
32 devices in a mesh: row: 4 (over z), col: 8 (over y, x, core).
Axes of the slice: x: 2, y: 2, z: 4, core: 2. Of those that a mesh axis runs over, the one named last changes fastest.
Arguments:
- frames: float32 [512, 64, 1024], P(('row', 'col')), may hold values from -1 to 6
- class_index: int32 [64, 1024], P('row', 'col'), may hold values from 0 to 7
- surface_mask: int32 [64, 1024], P('row', 'col'), may hold values 0 or 1
- effusivity: float32 [8], replicated, may hold values from 0.5 to 2
- conductivity: float32 [8], replicated, may hold values from 0.2 to 1
Outputs:
- heat_flux: float32 [64, 1024, 512], P('row', 'col')
All inputs are finite; a program needn't handle non-finite values. No bound on the sum of `surface_mask` on one device may be relied on, other than what follows from the above.
Results may differ from a plain program's by a relative error of at most 0.0003.
Values sent between devices are 32-bit elements; how exact they have to be, the bound alone decides.
A program may use at most 64 MiB of HBM per device.

v0:
```python
import jax
import jax.numpy as jnp
from jax import lax
from jax.sharding import PartitionSpec as P

PASSES = 3


flux_factor = 1.1283791670955126
lateral_rate = 0.24


def extended(block, sides, width):
    for axis, dim in sides:
        count = lax.axis_size(axis)
        forward = [(i, i + 1) for i in range(count - 1)]
        backward = [(target, source) for source, target in forward]
        low = lax.ppermute(
            lax.slice_in_dim(block, block.shape[dim] - width, None, axis=dim), axis, forward
        )
        high = lax.ppermute(lax.slice_in_dim(block, 0, width, axis=dim), axis, backward)
        block = jnp.concatenate([low, block, high], axis=dim)
    return block


def weights(lagged):
    clipped = jnp.maximum(lagged, 0.0)
    return jnp.where(lagged >= 0.0, 1.0 / (jnp.sqrt(clipped) + jnp.sqrt(clipped + 1.0)), 0.0)


def kernel_from(later, earlier):
    lagged = (later[:, None] - earlier[None, :]).astype(jnp.float32)
    return weights(lagged) - weights(lagged - 1.0)


def relax_once(padded, lateral):
    center = padded[1:-1, 1:-1]
    laplace = (
        padded[2:, 1:-1] + padded[:-2, 1:-1] + padded[1:-1, 2:] + padded[1:-1, :-2] - 4.0 * center
    )
    return center + lateral[:, :, None] * laplace


def per_device(frames, class_index, surface_mask, effusivity, conductivity):
    row_count = lax.axis_size("row")
    col_count = lax.axis_size("col")
    local_frames, height, width = frames.shape
    tile_rows = height // row_count
    tile_cols = width // col_count
    total_frames = local_frames * row_count * col_count
    frame_ids = jnp.arange(total_frames, dtype=jnp.int32)
    contract = (((0,), (1,)), ((), ()))
    kernel = kernel_from(frame_ids, frame_ids)
    blocks = frames.reshape(local_frames, row_count, tile_rows, col_count, tile_cols)
    blocks = blocks.transpose(0, 1, 3, 2, 4).reshape(
        local_frames, row_count * col_count, tile_rows, tile_cols
    )
    convolved = lax.dot_general(
        lax.all_to_all(blocks, ("row", "col"), split_axis=1, concat_axis=0, tiled=True)[:, 0],
        kernel,
        contract,
        precision=lax.Precision.HIGHEST,
    )
    classes = jnp.arange(effusivity.shape[0], dtype=jnp.int32)
    matches = (class_index[:, :, None] == classes[None, None, :]).astype(jnp.float32)
    maskf = surface_mask.astype(jnp.float32)
    gain = flux_factor * jnp.sum(matches * effusivity, axis=-1) * maskf
    lateral = lateral_rate * jnp.sum(matches * conductivity, axis=-1) * maskf
    heat_flux = convolved * gain[:, :, None]
    padded = extended(heat_flux, (("row", 0), ("col", 1)), PASSES)
    lateral_wide = extended(lateral, (("row", 0), ("col", 1)), PASSES - 1)
    for pass_index in range(PASSES):
        margin = PASSES - 1 - pass_index
        offset = PASSES - 1 - margin
        lateral_part = lateral_wide[
            offset : offset + tile_rows + 2 * margin, offset : offset + tile_cols + 2 * margin
        ]
        padded = relax_once(padded, lateral_part)
    heat_flux = padded
    return heat_flux


def solution(mesh):
    in_specs = (P(("row", "col"), None, None), P("row", "col"), P("row", "col"), P(), P())
    out_specs = P("row", "col", None)
    return jax.shard_map(
        per_device, mesh=mesh, in_specs=in_specs, out_specs=out_specs, check_vma=False
    )
```

profile of v0, /device:TPU:19, one launch (start us, length us, event | category | flops | bytes accessed | tf_op | source)
XLA Modules:
  0.0 172.4 jit_solution(1306813923509590767)
XLA Ops:
  0.0 3.2 %copy.11 = f32[128,8,8,128]{3,2,1,0:T(8,128)S(1)} copy(f32[128,8,8,128]{3,1,2,0:T(8,128)} %bitcast.20) | data formatting | bytes 8388608
  3.2 2.8 %copy.9 = f32[16,4,16,8,128]{4,2,0,3,1:T(8,128)} copy(f32[16,4,16,8,128]{4,3,2,1,0:T(8,128)S(1)} %bitcast.18) | data formatting | bytes 8388608 | tf_op jit(solution)/shard_map/reshape | solution.py:54
  6.0 0.0 copy-start
  6.0 0.0 copy-start.2
  6.0 0.0 copy-start.3
  6.0 0.0 copy-start.1
  6.0 6.3 %all-to-all-start = ((f32[16,32,16,128]{3,2,0,1:T(8,128)}), f32[16,32,16,128]{3,2,0,1:T(8,128)}, u32[]{:S(2)}, u32[]{:S(2)}) async-start(f32[16,32,16,128]{3,2,0,1:T(8,128)} %bitcast.17), calls=%async_computation | async-start | bytes 8388608 | tf_op jit(solution)/shard_map/all_to_all | solution.py:59
  12.2 0.0 copy-done
  12.2 0.0 copy-done.2
  12.2 0.0 copy-done.3
  12.3 0.1 select_reduce_fusion
  12.4 0.0 copy-done.1
  12.4 89.8 %all-to-all-done = f32[16,32,16,128]{3,2,0,1:T(8,128)} async-done(((f32[16,32,16,128]{3,2,0,1:T(8,128)}), f32[16,32,16,128]{3,2,0,1:T(8,128)}, u32[]{:S(2)}, u32[]{:S(2)}) %all-to-all-start) | async-done | bytes 4194336 | tf_op jit(solution)/shard_map/all_to_all | solution.py:59
  102.2 5.2 %copy.10 = f32[512,16,128]{0,2,1:T(8,128)} copy(f32[512,16,128]{2,1,0:T(8,128)} %bitcast.4) | data formatting | bytes 8388608 | tf_op jit(solution)/shard_map/squeeze | solution.py:59
  107.5 12.1 %fusion.9 = f32[512,2048]{0,1:S(1)} fusion(f32[512,2048]{0,1:T(8,128)} %bitcast.21), kind=kOutput, calls=%fused_computation.20 | convolution fusion | flops 6446645248 | bytes 8388608
  119.6 0.4 multiply_bitcast_fusion
  119.9 0.1 fusion.37
  120.1 4.1 %collective-permute-start = (f32[3,128,512]{2,1,0:T(8,128)S(1)}, f32[3,128,512]{2,1,0:T(8,128)S(1)}, u32[]{:S(2)}, u32[]{:S(2)}) collective-permute-start(f32[3,128,512]{2,1,0:T(8,128)S(1)} %get-tuple-element.9), channel_id=1, source_target_pairs={{0,8},{8,16},{16,24},{1,9},{9,17},{17,25},{2,10},{10,18},{18,26},{... | collective-permute-start | bytes 2359304 | tf_op jit(solution)/shard_map/ppermute | solution.py:18
  124.2 1.9 %collective-permute-start.1 = (f32[3,128,512]{2,1,0:T(8,128)S(1)}, f32[3,128,512]{2,1,0:T(8,128)S(1)}, u32[]{:S(2)}, u32[]{:S(2)}) collective-permute-start(f32[3,128,512]{2,1,0:T(8,128)S(1)} %get-tuple-element.10), channel_id=1, source_target_pairs={{8,0},{16,8},{24,16},{9,1},{17,9},{25,17},{10,2},{18,10},{26,18},{... | collective-permute-start | bytes 2359304 | tf_op jit(solution)/shard_map/ppermute | solution.py:21
  126.2 3.4 %collective-permute-start.4 = (f32[2,128]{1,0:T(2,128)S(1)}, f32[2,128]{1,0:T(2,128)S(1)}, u32[]{:S(2)}, u32[]{:S(2)}) collective-permute-start(f32[2,128]{1,0:T(2,128)S(1)} %get-tuple-element.13), channel_id=1, source_target_pairs={{0,8},{8,16},{16,24},{1,9},{9,17},{17,25},{2,10},{10,18},{18,26},{... | collective-permute-start | bytes 3080 | tf_op jit(solution)/shard_map/ppermute | solution.py:18
  129.6 1.9 %collective-permute-start.5 = (f32[2,128]{1,0:T(2,128)S(1)}, f32[2,128]{1,0:T(2,128)S(1)}, u32[]{:S(2)}, u32[]{:S(2)}) collective-permute-start(f32[2,128]{1,0:T(2,128)S(1)} %get-tuple-element.14), channel_id=1, source_target_pairs={{8,0},{16,8},{24,16},{9,1},{17,9},{25,17},{10,2},{18,10},{26,18},{... | collective-permute-start | bytes 3080 | tf_op jit(solution)/shard_map/ppermute | solution.py:21
  131.5 8.6 %collective-permute-done.4 = f32[2,128]{1,0:T(2,128)S(1)} collective-permute-done((f32[2,128]{1,0:T(2,128)S(1)}, f32[2,128]{1,0:T(2,128)S(1)}, u32[]{:S(2)}, u32[]{:S(2)}) %collective-permute-start.4) | collective-permute-done | bytes 1056 | tf_op jit(solution)/shard_map/ppermute | solution.py:18
  140.1 3.8 %collective-permute-done.5 = f32[2,128]{1,0:T(2,128)S(1)} collective-permute-done((f32[2,128]{1,0:T(2,128)S(1)}, f32[2,128]{1,0:T(2,128)S(1)}, u32[]{:S(2)}, u32[]{:S(2)}) %collective-permute-start.5) | collective-permute-done | bytes 1056 | tf_op jit(solution)/shard_map/ppermute | solution.py:21
  144.0 0.0 collective-permute-done
  144.0 0.0 collective-permute-done.1
  144.0 0.1 pad_maximum_fusion.3
  144.1 5.6 %collective-permute-start.2 = (f32[22,3,512]{2,1,0:T(4,128)S(1)}, f32[22,3,512]{2,1,0:T(4,128)S(1)}, u32[]{:S(2)}, u32[]{:S(2)}) collective-permute-start(f32[22,3,512]{2,1,0:T(4,128)S(1)} %get-tuple-element.7), channel_id=1, source_target_pairs={{0,1},{1,2},{2,3},{3,4},{4,5},{5,6},{6,7},{8,9},{9,10},{10,11},{11... | collective-permute-start | bytes 405512 | tf_op jit(solution)/shard_map/ppermute | solution.py:18
  149.7 1.9 %collective-permute-start.3 = (f32[22,3,512]{2,1,0:T(4,128)S(1)}, f32[22,3,512]{2,1,0:T(4,128)S(1)}, u32[]{:S(2)}, u32[]{:S(2)}) collective-permute-start(f32[22,3,512]{2,1,0:T(4,128)S(1)} %get-tuple-element.8), channel_id=1, source_target_pairs={{1,0},{2,1},{3,2},{4,3},{5,4},{6,5},{7,6},{9,8},{10,9},{11,10},{12... | collective-permute-start | bytes 405512 | tf_op jit(solution)/shard_map/ppermute | solution.py:21
  151.6 0.1 fusion.38
  151.7 4.5 %collective-permute-start.6 = (f32[20,2]{1,0:T(8,128)S(1)}, f32[20,2]{1,0:T(8,128)S(1)}, u32[]{:S(2)}, u32[]{:S(2)}) collective-permute-start(f32[20,2]{1,0:T(8,128)S(1)} %get-tuple-element.11), channel_id=1, source_target_pairs={{0,1},{1,2},{2,3},{3,4},{4,5},{5,6},{6,7},{8,9},{9,10},{10,11},{11... | collective-permute-start | bytes 488 | tf_op jit(solution)/shard_map/ppermute | solution.py:18
  156.2 2.1 %collective-permute-start.7 = (f32[20,2]{1,0:T(8,128)S(1)}, f32[20,2]{1,0:T(8,128)S(1)}, u32[]{:S(2)}, u32[]{:S(2)}) collective-permute-start(f32[20,2]{1,0:T(8,128)S(1)} %get-tuple-element.12), channel_id=1, source_target_pairs={{1,0},{2,1},{3,2},{4,3},{5,4},{6,5},{7,6},{9,8},{10,9},{11,10},{12... | collective-permute-start | bytes 488 | tf_op jit(solution)/shard_map/ppermute | solution.py:21
  158.3 0.0 collective-permute-done.6
  158.3 3.8 %collective-permute-done.7 = f32[20,2]{1,0:T(8,128)S(1)} collective-permute-done((f32[20,2]{1,0:T(8,128)S(1)}, f32[20,2]{1,0:T(8,128)S(1)}, u32[]{:S(2)}, u32[]{:S(2)}) %collective-permute-start.7) | collective-permute-done | bytes 192 | tf_op jit(solution)/shard_map/ppermute | solution.py:21
  162.1 0.1 pad_maximum_fusion.4
  162.2 0.1 slice.108
  162.3 0.0 collective-permute-done.2
  162.3 0.0 collective-permute-done.3
  162.3 1.1 pad_maximum_fusion
  163.4 2.8 %fusion.2 = f32[20,132,512]{2,1,0:T(8,128)S(1)} fusion(f32[22,134,512]{2,1,0:T(8,128)S(1)} %pad_maximum_fusion, f32[20,132]{1,0:T(8,128)S(1)} %pad_maximum_fusion.4), kind=kLoop, calls=%fused_computation.4 | loop fusion | flops 9461760 | bytes 32450880 | tf_op jit(solution)/shard_map/add | solution.py:41
  166.2 2.8 %fusion.5 = f32[18,130,512]{2,1,0:T(8,128)S(1)} fusion(f32[20,132,512]{2,1,0:T(8,128)S(1)} %fusion.2, f32[18,130]{1,0:T(8,128)S(1)} %slice.108), kind=kLoop, calls=%fused_computation.10 | loop fusion | flops 8386560 | bytes 28763280 | tf_op jit(solution)/shard_map/add | solution.py:41
  169.0 3.4 %fusion.8 = f32[16,128,512]{2,1,0:T(8,128)} fusion(f32[18,130,512]{2,1,0:T(8,128)S(1)} %fusion.5, f32[16,128]{1,0:T(8,128)S(1)} %get-tuple-element.15), kind=kLoop, calls=%fused_computation.16 | loop fusion | flops 7340032 | bytes 25174016 | tf_op jit(solution)/shard_map/add | solution.py:41
  (3 shorter events, 0.0 us)
Async XLA Ops:
  6.0 6.3 %copy-start = (s32[16,128]{1,0:T(8,128)S(1)}, s32[16,128]{1,0:T(8,128)}, u32[]{:S(2)}) copy-start(s32[16,128]{1,0:T(8,128)} %param.6) | copy-start | bytes 24580
  6.0 6.3 %copy-start.2 = (f32[8]{0:T(128)S(1)}, f32[8]{0:T(128)}, u32[]{:S(2)}) copy-start(f32[8]{0:T(128)} %param.9) | copy-start | bytes 100
  6.0 6.3 %copy-start.3 = (f32[8]{0:T(128)S(1)}, f32[8]{0:T(128)}, u32[]{:S(2)}) copy-start(f32[8]{0:T(128)} %param.8) | copy-start | bytes 100
  6.0 6.4 %copy-start.1 = (s32[16,128]{1,0:T(8,128)S(1)}, s32[16,128]{1,0:T(8,128)}, u32[]{:S(2)}) copy-start(s32[16,128]{1,0:T(8,128)} %param.7) | copy-start | bytes 24580
  6.0 96.3 %all-to-all-start = ((f32[16,32,16,128]{3,2,0,1:T(8,128)}), f32[16,32,16,128]{3,2,0,1:T(8,128)}, u32[]{:S(2)}, u32[]{:S(2)}) async-start(f32[16,32,16,128]{3,2,0,1:T(8,128)} %bitcast.17), calls=%async_computation | async-start | bytes 8388608 | tf_op jit(solution)/shard_map/all_to_all | solution.py:59
  120.1 23.9 %collective-permute-start = (f32[3,128,512]{2,1,0:T(8,128)S(1)}, f32[3,128,512]{2,1,0:T(8,128)S(1)}, u32[]{:S(2)}, u32[]{:S(2)}) collective-permute-start(f32[3,128,512]{2,1,0:T(8,128)S(1)} %get-tuple-element.9), channel_id=1, source_target_pairs={{0,8},{8,16},{16,24},{1,9},{9,17},{17,25},{2,10},{10,18},{18,26},{... | collective-permute-start | bytes 2359304 | tf_op jit(solution)/shard_map/ppermute | solution.py:18
  124.2 19.8 %collective-permute-start.1 = (f32[3,128,512]{2,1,0:T(8,128)S(1)}, f32[3,128,512]{2,1,0:T(8,128)S(1)}, u32[]{:S(2)}, u32[]{:S(2)}) collective-permute-start(f32[3,128,512]{2,1,0:T(8,128)S(1)} %get-tuple-element.10), channel_id=1, source_target_pairs={{8,0},{16,8},{24,16},{9,1},{17,9},{25,17},{10,2},{18,10},{26,18},{... | collective-permute-start | bytes 2359304 | tf_op jit(solution)/shard_map/ppermute | solution.py:21
  126.2 14.0 %collective-permute-start.4 = (f32[2,128]{1,0:T(2,128)S(1)}, f32[2,128]{1,0:T(2,128)S(1)}, u32[]{:S(2)}, u32[]{:S(2)}) collective-permute-start(f32[2,128]{1,0:T(2,128)S(1)} %get-tuple-element.13), channel_id=1, source_target_pairs={{0,8},{8,16},{16,24},{1,9},{9,17},{17,25},{2,10},{10,18},{18,26},{... | collective-permute-start | bytes 3080 | tf_op jit(solution)/shard_map/ppermute | solution.py:18
  129.6 14.4 %collective-permute-start.5 = (f32[2,128]{1,0:T(2,128)S(1)}, f32[2,128]{1,0:T(2,128)S(1)}, u32[]{:S(2)}, u32[]{:S(2)}) collective-permute-start(f32[2,128]{1,0:T(2,128)S(1)} %get-tuple-element.14), channel_id=1, source_target_pairs={{8,0},{16,8},{24,16},{9,1},{17,9},{25,17},{10,2},{18,10},{26,18},{... | collective-permute-start | bytes 3080 | tf_op jit(solution)/shard_map/ppermute | solution.py:21
  144.1 18.2 %collective-permute-start.2 = (f32[22,3,512]{2,1,0:T(4,128)S(1)}, f32[22,3,512]{2,1,0:T(4,128)S(1)}, u32[]{:S(2)}, u32[]{:S(2)}) collective-permute-start(f32[22,3,512]{2,1,0:T(4,128)S(1)} %get-tuple-element.7), channel_id=1, source_target_pairs={{0,1},{1,2},{2,3},{3,4},{4,5},{5,6},{6,7},{8,9},{9,10},{10,11},{11... | collective-permute-start | bytes 405512 | tf_op jit(solution)/shard_map/ppermute | solution.py:18
  149.7 12.6 %collective-permute-start.3 = (f32[22,3,512]{2,1,0:T(4,128)S(1)}, f32[22,3,512]{2,1,0:T(4,128)S(1)}, u32[]{:S(2)}, u32[]{:S(2)}) collective-permute-start(f32[22,3,512]{2,1,0:T(4,128)S(1)} %get-tuple-element.8), channel_id=1, source_target_pairs={{1,0},{2,1},{3,2},{4,3},{5,4},{6,5},{7,6},{9,8},{10,9},{11,10},{12... | collective-permute-start | bytes 405512 | tf_op jit(solution)/shard_map/ppermute | solution.py:21
  151.7 6.7 %collective-permute-start.6 = (f32[20,2]{1,0:T(8,128)S(1)}, f32[20,2]{1,0:T(8,128)S(1)}, u32[]{:S(2)}, u32[]{:S(2)}) collective-permute-start(f32[20,2]{1,0:T(8,128)S(1)} %get-tuple-element.11), channel_id=1, source_target_pairs={{0,1},{1,2},{2,3},{3,4},{4,5},{5,6},{6,7},{8,9},{9,10},{10,11},{11... | collective-permute-start | bytes 488 | tf_op jit(solution)/shard_map/ppermute | solution.py:18
  156.2 5.9 %collective-permute-start.7 = (f32[20,2]{1,0:T(8,128)S(1)}, f32[20,2]{1,0:T(8,128)S(1)}, u32[]{:S(2)}, u32[]{:S(2)}) collective-permute-start(f32[20,2]{1,0:T(8,128)S(1)} %get-tuple-element.12), channel_id=1, source_target_pairs={{1,0},{2,1},{3,2},{4,3},{5,4},{6,5},{7,6},{9,8},{10,9},{11,10},{12... | collective-permute-start | bytes 488 | tf_op jit(solution)/shard_map/ppermute | solution.py:21
where the time goes:
time: 173 us; the launch traced here: 172 us
  waiting for transfers between devices  106 us (61%)
  starting transfers between devices  31.8 us (18%)
  matrix products  12.1 us (7%)
  local copies, waits for them, and re-layouts  11.5 us (7%)
  other arithmetic  10.7 us (6%)
    all_to_all x1, waiting for transfers between devices, per_device(): lax.all_to_all(blocks, ('row', 'col'), split_axis=1, concat_axis=0, tiled...  89.8 us
    ppermute x4, starting transfers between devices, extended(): lax.ppermute(lax.slice_in_dim(block, block.shape[dim] - width, None, axis...  17.6 us
    unnamed x1, matrix products  12.1 us
    add x3, other arithmetic, relax_once(): return center + lateral[:, :, None] * laplace  9.04 us
    ppermute x4, waiting for transfers between devices, extended(): lax.ppermute(lax.slice_in_dim(block, block.shape[dim] - width, None, axis...  8.64 us
    ppermute x4, starting transfers between devices, extended(): lax.ppermute(lax.slice_in_dim(block, 0, width, axis=dim), axis, backward)  7.86 us
    ppermute x4, waiting for transfers between devices, extended(): lax.ppermute(lax.slice_in_dim(block, 0, width, axis=dim), axis, backward)  7.64 us
    all_to_all x1, starting transfers between devices, per_device(): lax.all_to_all(blocks, ('row', 'col'), split_axis=1, concat_axis=0, tiled...  6.25 us
  transfers between devices with their start and end apart: 9, of which 4 were waited for; matrix products, arithmetic and copies ran while one was open for 0% of the time, Pallas kernels for 0%

commit v1 on v0

--- a/solution.py
+++ b/solution.py
@@ -1,10 +1,16 @@
+import functools
 import jax
 import jax.numpy as jnp
 from jax import lax
+from jax.experimental import pallas as pl
+from jax.experimental.pallas import tpu as pltpu
 from jax.sharding import PartitionSpec as P
 
 PASSES = 3
-
+PAD = 8
+GROUP = 8
+LANES = 128
+MESH = pl.DeviceIdType.MESH
 
 flux_factor = 1.1283791670955126
 lateral_rate = 0.24
@@ -41,7 +47,7 @@
     return center + lateral[:, :, None] * laplace
 
 
-def per_device(frames, class_index, surface_mask, effusivity, conductivity):
+def plain_device(frames, class_index, surface_mask, effusivity, conductivity):
     row_count = lax.axis_size("row")
     col_count = lax.axis_size("col")
     local_frames, height, width = frames.shape
@@ -76,8 +82,281 @@
             offset : offset + tile_rows + 2 * margin, offset : offset + tile_cols + 2 * margin
         ]
         padded = relax_once(padded, lateral_part)
-    heat_flux = padded
-    return heat_flux
+    return padded
+
+
+SIDES = ((-1, 0), (1, 0), (0, -1), (0, 1), (-1, -1), (-1, 1), (1, -1), (1, 1))
+
+
+def gather_kernel(
+    rows, cols, tile_rows, tile_cols, local,
+    frames, class_ref, mask_ref, eff_ref, cond_ref,
+    flux, wide,
+    held, lat, near, gain, mix_ref,
+    send_sem, recv_sem, own_sem, lat_send, lat_recv, halo_send, halo_recv,
+):
+    row, col = lax.axis_index("row"), lax.axis_index("col")
+    group = cols * local
+    total = rows * group
+    halo = PASSES
+
+    def there(step, count, at):
+        return (at + step >= 0) & (at + step < count)
+
+    def exists(side):
+        return there(side[0], rows, row) & there(side[1], cols, col)
+
+    classes = class_ref[...]
+    maskf = mask_ref[...].astype(jnp.float32)
+    eff = jnp.zeros(classes.shape, jnp.float32)
+    cond = jnp.zeros(classes.shape, jnp.float32)
+    for k in range(eff_ref.shape[0]):
+        eff = jnp.where(classes == k, eff_ref[k], eff)
+        cond = jnp.where(classes == k, cond_ref[k], cond)
+    gain_rows = flux_factor * eff * maskf
+    lat_rows = lateral_rate * cond * maskf
+    lat[...] = lat_rows
+    near[...] = jnp.zeros_like(near)
+
+    @pl.loop(0, tile_rows + 2 * halo)
+    def _(h):
+        flux[h] = jnp.zeros(flux.shape[1:], jnp.float32)
+
+    barrier = pltpu.get_barrier_semaphore()
+    for k in range(rows):
+        @pl.loop(0 if k else 1, cols)
+        def _(j, k=k):
+            pl.semaphore_signal(
+                barrier, inc=1,
+                device_id=(lax.rem(row + k, rows), lax.rem(col + j, cols)),
+                device_id_type=MESH,
+            )
+    pl.semaphore_wait(barrier, rows * cols - 1)
+
+    def lat_copy(i):
+        side = SIDES[i]
+        return pltpu.make_async_remote_copy(
+            src_ref=lat, dst_ref=near.at[i], send_sem=lat_send.at[i], recv_sem=lat_recv.at[i],
+            device_id=(row + side[0], col + side[1]), device_id_type=MESH,
+        )
+
+    order = [rows // 2] + [k for k in range(rows) if k != rows // 2 and k] + [0]
+    order = list(dict.fromkeys(order))
+    for k in order:
+        @pl.loop(0 if k else 1, cols)
+        def _(j, k=k):
+            to_row, to_col = lax.rem(row + k, rows), lax.rem(col + j, cols)
+            pltpu.make_async_remote_copy(
+                src_ref=frames.at[
+                    :,
+                    pl.ds(pl.multiple_of(to_row * tile_rows, tile_rows), tile_rows),
+                    pl.ds(pl.multiple_of(to_col * tile_cols, tile_cols), tile_cols),
+                ],
+                dst_ref=held.at[pl.ds((row * cols + col) * local, local)],
+                send_sem=send_sem, recv_sem=recv_sem.at[k],
+                device_id=(to_row, to_col), device_id_type=MESH,
+            ).start()
+        if k == order[0]:
+            for i, side in enumerate(SIDES):
+                @pl.when(exists(side))
+                def _(i=i):
+                    lat_copy(i).start()
+    own = pltpu.make_async_copy(
+        frames.at[
+            :,
+            pl.ds(pl.multiple_of(row * tile_rows, tile_rows), tile_rows),
+            pl.ds(pl.multiple_of(col * tile_cols, tile_cols), tile_cols),
+        ],
+        held.at[pl.ds((row * cols + col) * local, local)],
+        own_sem,
+    )
+    own.start()
+
+    for k in range(rows):
+        shape = (group, total)
+        earlier = lax.broadcasted_iota(jnp.int32, shape, 0) + k * group
+        later = lax.broadcasted_iota(jnp.int32, shape, 1)
+        lagged = (later - earlier).astype(jnp.float32)
+        mix = weights(lagged) - weights(lagged - 1.0)
+        high = mix.astype(jnp.bfloat16)
+        mix_ref[0, k * group : (k + 1) * group] = high
+        mix_ref[1, k * group : (k + 1) * group] = (mix - high.astype(jnp.float32)).astype(jnp.bfloat16)
+
+    def upright(line):
+        return jnp.transpose(jnp.broadcast_to(line, (tile_cols, tile_cols)))[:, :LANES]
+
+    for h in range(tile_rows):
+        gain[h] = upright(gain_rows[h : h + 1])
+    for i, side in enumerate(SIDES):
+        @pl.when(exists((-side[0], -side[1])))
+        def _(i=i):
+            lat_copy(i).wait_recv()
+        @pl.when(exists(side))
+        def _(i=i):
+            lat_copy(i).wait_send()
+    slot = {(-a, -b): i for i, (a, b) in enumerate(SIDES)}
+    inside = slice(PAD, PAD + tile_cols)
+    for h in range(-halo, tile_rows + halo):
+        up = -1 if h < 0 else (1 if h >= tile_rows else 0)
+        at = h - up * tile_rows
+        def line(side):
+            if side == (0, 0):
+                return lat_rows[at : at + 1]
+            return near[slot[side], at : at + 1, :]
+        wide[h + halo, inside] = upright(line((up, 0)))
+        wide[h + halo, 0:PAD] = upright(line((up, -1)))[tile_cols - PAD :]
+        wide[h + halo, PAD + tile_cols :] = upright(line((up, 1)))[:PAD]
+
+    def product(source, q):
+        x = held[pl.ds(pl.multiple_of(source * group, group), group), q * GROUP : (q + 1) * GROUP, :]
+        x = jnp.transpose(jnp.swapaxes(x, 0, 1), (0, 2, 1)).reshape(GROUP * tile_cols, group)
+        high = x.astype(jnp.bfloat16)
+        low = (x - high.astype(jnp.float32)).astype(jnp.bfloat16)
+        at = pl.ds(pl.multiple_of(source * group, group), group)
+        out = jnp.dot(high, mix_ref[0, at], preferred_element_type=jnp.float32)
+        out += jnp.dot(low, mix_ref[0, at], preferred_element_type=jnp.float32)
+        out += jnp.dot(high, mix_ref[1, at], preferred_element_type=jnp.float32)
+        return out.reshape(GROUP, tile_cols, total)
+
+    def part(q):
+        return slice(halo + q * GROUP, halo + (q + 1) * GROUP)
+
+    def arrived(k):
+        if k == 0:
+            own.wait()
+            blocks = held.at[pl.ds(0, group - local)]
+        else:
+            blocks = held.at[pl.ds(0, group)]
+        pltpu.make_async_copy(blocks, blocks, recv_sem.at[k]).wait()
+        return lax.rem(row - k + rows, rows)
+
+    visits = [k for k in order if k]
+    visits = visits[:-1] + [0] + visits[-1:]
+    for k in visits[:-1]:
+        source = arrived(k)
+        for q in range(tile_rows // GROUP):
+            flux[part(q), inside] += product(source, q)
+
+    col_spans = {-1: (PAD, PAD + tile_cols), 1: (tile_cols, 0)}
+
+    def halo_copy(i):
+        up, aside = SIDES[i]
+        near_rows = halo if aside == 0 else halo - 1
+        if up == 0:
+            from_rows = to_rows = pl.ds(halo, tile_rows)
+        elif up < 0:
+            from_rows, to_rows = pl.ds(halo, near_rows), pl.ds(halo + tile_rows, near_rows)
+        else:
+            from_rows = pl.ds(halo + tile_rows - near_rows, near_rows)
+            to_rows = pl.ds(halo - near_rows, near_rows)
+        if aside == 0:
+            from_cols = to_cols = pl.ds(PAD, tile_cols)
+        else:
+            from_cols = pl.ds(col_spans[aside][0], PAD)
+            to_cols = pl.ds(col_spans[aside][1], PAD)
+        return pltpu.make_async_remote_copy(
+            src_ref=flux.at[from_rows, from_cols], dst_ref=flux.at[to_rows, to_cols],
+            send_sem=halo_send.at[i], recv_sem=halo_recv.at[i],
+            device_id=(row + up, col + aside), device_id_type=MESH,
+        )
+
+    def send_halo(i):
+        @pl.when(exists(SIDES[i]))
+        def _():
+            halo_copy(i).start()
+
+    source = arrived(visits[-1])
+    last = tile_rows // GROUP - 1
+    for q in range(last + 1):
+        here = slice(q * GROUP, (q + 1) * GROUP)
+        g = jnp.concatenate([gain[here]] * (total // LANES), axis=-1)
+        flux[part(q), inside] = (flux[part(q), inside] + product(source, q)) * g
+        for i, side in enumerate(SIDES):
+            if (side[0] == -1 and q == 0) or (side[0] == 1 and q == last):
+                send_halo(i)
+    for i, side in enumerate(SIDES):
+        if side[0] == 0:
+            send_halo(i)
+
+    sent = held.at[pl.ds(0, total - local)]
+    pltpu.make_async_copy(sent, sent, send_sem).wait()
+    for i, side in enumerate(SIDES):
+        @pl.when(exists(side))
+        def _(i=i):
+            halo_copy(i).wait_send()
+        @pl.when(exists((-side[0], -side[1])))
+        def _(i=i):
+            halo_copy(i).wait_recv()
+
+
+def relax_kernel(flux, wide, out, first, second):
+    source = flux
+    count, width = flux.shape[0], flux.shape[1]
+    for step, target in enumerate((first, second, out)):
+        low, high = step + 1, count - step - 1
+        edge = (1 + step, width - 1 - step) if target is not out else (PAD, width - PAD)
+        for h in range(low, high):
+            a, b = edge
+            center = source[h, a:b, :]
+            laplace = (
+                source[h + 1, a:b, :] + source[h - 1, a:b, :]
+                + source[h, a + 1 : b + 1, :] + source[h, a - 1 : b - 1, :] - 4.0 * center
+            )
+            value = center + wide[h, a:b, :] * laplace
+            if target is out:
+                out[h - PASSES] = value
+            else:
+                target[h, a:b, :] = value
+        source = target
+
+
+def per_device(frames, class_index, surface_mask, effusivity, conductivity):
+    rows = lax.axis_size("row")
+    cols = lax.axis_size("col")
+    local, height, width = frames.shape
+    tile_rows, tile_cols = height // rows, width // cols
+    total = local * rows * cols
+    if local % 8 or tile_rows % GROUP or tile_cols != LANES or total % LANES or (local * cols) % LANES:
+        return plain_device(frames, class_index, surface_mask, effusivity, conductivity)
+    high_rows, wide_cols = tile_rows + 2 * PASSES, tile_cols + 2 * PAD
+    vmem = pl.BlockSpec(memory_space=pltpu.VMEM)
+    smem = pl.BlockSpec(memory_space=pltpu.SMEM)
+    dma = pltpu.SemaphoreType.DMA
+    sides = len(SIDES)
+    flux, wide = pl.pallas_call(
+        functools.partial(gather_kernel, rows, cols, tile_rows, tile_cols, local),
+        out_shape=(
+            jax.ShapeDtypeStruct((high_rows, wide_cols, total), jnp.float32),
+            jax.ShapeDtypeStruct((high_rows, wide_cols, LANES), jnp.float32),
+        ),
+        in_specs=[pl.BlockSpec(memory_space=pltpu.HBM), vmem, vmem, smem, smem],
+        out_specs=(vmem, vmem),
+        scratch_shapes=[
+            pltpu.VMEM((total, tile_rows, tile_cols), jnp.float32),
+            pltpu.VMEM((tile_rows, tile_cols), jnp.float32),
+            pltpu.VMEM((sides, tile_rows, tile_cols), jnp.float32),
+            pltpu.VMEM((tile_rows, tile_cols, LANES), jnp.float32),
+            pltpu.VMEM((2, total, total), jnp.bfloat16),
+            dma, dma((rows,)), dma, dma((sides,)), dma((sides,)), dma((sides,)), dma((sides,)),
+        ],
+        compiler_params=pltpu.CompilerParams(
+            collective_id=0, has_side_effects=True, vmem_limit_bytes=40 * 2**20
+        ),
+        name="gather",
+    )(frames, class_index, surface_mask, effusivity, conductivity)
+    return pl.pallas_call(
+        relax_kernel,
+        out_shape=jax.ShapeDtypeStruct((tile_rows, tile_cols, total), jnp.float32),
+        grid=(total // LANES,),
+        in_specs=[
+            pl.BlockSpec((high_rows, wide_cols, LANES), lambda n: (0, 0, n)),
+            pl.BlockSpec((high_rows, wide_cols, LANES), lambda n: (0, 0, 0)),
+        ],
+        out_specs=pl.BlockSpec((tile_rows, tile_cols, LANES), lambda n: (0, 0, n)),
+        scratch_shapes=[pltpu.VMEM((high_rows, wide_cols, LANES), jnp.float32)] * 2,
+        compiler_params=pltpu.CompilerParams(vmem_limit_bytes=24 * 2**20),
+        name="relax",
+    )(flux, wide)
 
 
 def solution(mesh):

time: 173 us -> 135 us (0.78)
  Pallas kernels: 0 us -> 128 us
  waiting for transfers between devices: 106 us -> 0 us
  starting transfers between devices: 31.8 us -> 0 us
  matrix products: 12.1 us -> 0 us
  other arithmetic: 10.7 us -> 0 us
  local copies, waits for them, and re-layouts: 11.5 us -> 4.89 us
    pallas_call x0 -> x2, Pallas kernels: none -> 128 us  [the longest x1 122 us: per_device(): pl.pallas_call(functools.partial(gather_kernel, rows, cols, tile_rows, ti...]
    all_to_all x1 -> x0, waiting for transfers between devices: 89.8 us -> none  [per_device(): lax.all_to_all(blocks, ('row', 'col'), split_axis=1, concat_axis=0, tiled...]
    ppermute x8 -> x0, starting transfers between devices: 25.5 us -> none  [the longest x4 17.6 us: extended(): lax.ppermute(lax.slice_in_dim(block, block.shape[dim] - width, None, axis...]
    ppermute x8 -> x0, waiting for transfers between devices: 16.3 us -> none  [the longest x4 8.64 us: extended(): lax.ppermute(lax.slice_in_dim(block, block.shape[dim] - width, None, axis...]
    unnamed x1 -> x0, matrix products: 12.1 us -> none
    add x3 -> x0, other arithmetic: 9.04 us -> none  [relax_once(): return center + lateral[:, :, None] * laplace]
    all_to_all x1 -> x0, starting transfers between devices: 6.25 us -> none  [per_device(): lax.all_to_all(blocks, ('row', 'col'), split_axis=1, concat_axis=0, tiled...]
    squeeze x1 -> x0, local copies, waits for them, and re-layouts: 5.23 us -> none  [per_device(): lax.all_to_all(blocks, ('row', 'col'), split_axis=1, concat_axis=0, tiled...]
  transfers between devices with their start and end apart: 9 -> 0, of which waited for: 4 -> 0; matrix products, arithmetic and copies ran while one was open for 0% -> 0% of each run, Pallas kernels for 0% -> 0%
where the time goes in v1:
time: 135 us; the launch traced here: 133 us
  Pallas kernels  128 us (95%)
  local copies, waits for them, and re-layouts  4.89 us (4%)
    pallas_call x1, Pallas kernels, per_device(): pl.pallas_call(functools.partial(gather_kernel, rows, cols, tile_rows, ti...  122 us
    pallas_call x1, Pallas kernels, per_device(): pl.pallas_call(relax_kernel, out_shape=jax.ShapeDtypeStruct((tile_rows, t...  6.42 us
    unnamed x10, local copies, waits for them, and re-layouts  4.89 us

profile of v1, /device:TPU:19, one launch (start us, length us, event | category | flops | bytes accessed | tf_op | source)
XLA Modules:
  0.0 133.3 jit_solution(10549328139652745376)
XLA Ops:
  0.0 0.0 copy-start
  0.0 2.2 %copy-done = f32[16,64,1024]{2,1,0:T(8,128)S(1)} copy-done((f32[16,64,1024]{2,1,0:T(8,128)S(1)}, f32[16,64,1024]{2,1,0:T(8,128)}, u32[]{:S(2)}) %copy-start) | copy-done | bytes 4194328
  2.2 0.0 copy-start.1
  2.2 0.7 copy-done.1
  2.9 0.0 copy-start.2
  2.9 0.7 copy-done.2
  3.6 0.0 copy-start.3
  3.6 0.7 copy-done.3
  4.2 0.0 copy-start.4
  4.2 0.7 copy-done.4
  4.9 122.0 %gather.1 = (f32[22,144,512]{2,1,0:T(8,128)S(1)}, f32[22,144,128]{2,1,0:T(8,128)S(1)}) custom-call(f32[16,64,1024]{2,1,0:T(8,128)S(1)} %copy-done, s32[16,128]{1,0:T(8,128)S(1)} %copy-done.1, s32[16,128]{1,0:T(8,128)S(1)} %copy-done.2, f32[8]{0:T(128)S(1)} %copy-done.3, f32[8]{0:T(128)S(1)} %copy-done.4), custom_call_target="tpu_custom_call" | custom-call | tf_op jit(solution)/shard_map/gather/pallas_call | solution.py:326
  126.9 6.4 %relax.1 = f32[16,128,512]{2,1,0:T(8,128)} custom-call(f32[22,144,512]{2,1,0:T(8,128)S(1)} %get-tuple-element.7.flux, f32[22,144,128]{2,1,0:T(8,128)S(1)} %get-tuple-element.8.wide), custom_call_target="tpu_custom_call" | custom-call | tf_op jit(solution)/shard_map/relax/pallas_call | solution.py:347
Async XLA Ops:
  0.0 2.2 %copy-start = (f32[16,64,1024]{2,1,0:T(8,128)S(1)}, f32[16,64,1024]{2,1,0:T(8,128)}, u32[]{:S(2)}) copy-start(f32[16,64,1024]{2,1,0:T(8,128)} %frames.1) | copy-start | bytes 12582916
  2.2 0.7 copy-start.1
  2.9 0.7 copy-start.2
  3.6 0.7 copy-start.3
  4.2 0.7 copy-start.4

commit v2 on v1

--- a/solution.py
+++ b/solution.py
@@ -92,13 +92,16 @@
     rows, cols, tile_rows, tile_cols, local,
     frames, class_ref, mask_ref, eff_ref, cond_ref,
     flux, wide,
-    held, lat, near, gain, mix_ref,
-    send_sem, recv_sem, own_sem, lat_send, lat_recv, halo_send, halo_recv,
+    held, lat, near, gain, mix_ref, edge, rim, strip, side_out, side_in,
+    send_sem, recv_sem, own_sem, lat_send, lat_recv,
+    strip_send, strip_recv, strip_own, relay_send, relay_recv, side_send, side_recv,
 ):
     row, col = lax.axis_index("row"), lax.axis_index("col")
     group = cols * local
     total = rows * group
     halo = PASSES
+    mid = rows // 2
+    half = row // mid
 
     def there(step, count, at):
         return (at + step >= 0) & (at + step < count)
@@ -115,7 +118,8 @@
         cond = jnp.where(classes == k, cond_ref[k], cond)
     gain_rows = flux_factor * eff * maskf
     lat_rows = lateral_rate * cond * maskf
-    lat[...] = lat_rows
+    lat[0] = lat_rows
+    lat[1] = gain_rows
     near[...] = jnp.zeros_like(near)
 
     @pl.loop(0, tile_rows + 2 * halo)
@@ -140,17 +144,17 @@
             device_id=(row + side[0], col + side[1]), device_id_type=MESH,
         )
 
+    def column(at):
+        return pl.ds(pl.multiple_of(at * tile_cols, tile_cols), tile_cols)
+
     order = [rows // 2] + [k for k in range(rows) if k != rows // 2 and k] + [0]
-    order = list(dict.fromkeys(order))
     for k in order:
         @pl.loop(0 if k else 1, cols)
         def _(j, k=k):
             to_row, to_col = lax.rem(row + k, rows), lax.rem(col + j, cols)
             pltpu.make_async_remote_copy(
                 src_ref=frames.at[
-                    :,
-                    pl.ds(pl.multiple_of(to_row * tile_rows, tile_rows), tile_rows),
-                    pl.ds(pl.multiple_of(to_col * tile_cols, tile_cols), tile_cols),
+                    :, pl.ds(pl.multiple_of(to_row * tile_rows, tile_rows), tile_rows), column(to_col)
                 ],
                 dst_ref=held.at[pl.ds((row * cols + col) * local, local)],
                 send_sem=send_sem, recv_sem=recv_sem.at[k],
@@ -162,15 +166,38 @@
                 def _(i=i):
                     lat_copy(i).start()
     own = pltpu.make_async_copy(
-        frames.at[
-            :,
-            pl.ds(pl.multiple_of(row * tile_rows, tile_rows), tile_rows),
-            pl.ds(pl.multiple_of(col * tile_cols, tile_cols), tile_cols),
-        ],
+        frames.at[:, pl.ds(pl.multiple_of(row * tile_rows, tile_rows), tile_rows), column(col)],
         held.at[pl.ds((row * cols + col) * local, local)],
         own_sem,
     )
     own.start()
+
+    strip_row = mid - 1 + half
+    strip_from = pl.ds(pl.multiple_of(mid * tile_rows - GROUP * half, GROUP), GROUP)
+    strip_at = strip.at[pl.ds(((row - half * mid) * cols + col) * local, local)]
+    beside = row == strip_row
+
+    def strip_copy(j):
+        to_col = lax.rem(col + j, cols)
+        return pltpu.make_async_remote_copy(
+            src_ref=frames.at[:, strip_from, column(to_col)], dst_ref=strip_at,
+            send_sem=strip_send, recv_sem=strip_recv.at[row - half * mid],
+            device_id=(strip_row, to_col), device_id_type=MESH,
+        )
+
+    @pl.loop(1, cols)
+    def _(j):
+        strip_copy(j).start()
+
+    strip_self = pltpu.make_async_copy(frames.at[:, strip_from, column(col)], strip_at, strip_own)
+
+    @pl.when(beside)
+    def _():
+        strip_self.start()
+
+    @pl.when(jnp.logical_not(beside))
+    def _():
+        strip_copy(0).start()
 
     for k in range(rows):
         shape = (group, total)
@@ -185,8 +212,6 @@
     def upright(line):
         return jnp.transpose(jnp.broadcast_to(line, (tile_cols, tile_cols)))[:, :LANES]
 
-    for h in range(tile_rows):
-        gain[h] = upright(gain_rows[h : h + 1])
     for i, side in enumerate(SIDES):
         @pl.when(exists((-side[0], -side[1])))
         def _(i=i):
@@ -199,94 +224,158 @@
     for h in range(-halo, tile_rows + halo):
         up = -1 if h < 0 else (1 if h >= tile_rows else 0)
         at = h - up * tile_rows
-        def line(side):
+        def line(side, which=0):
             if side == (0, 0):
-                return lat_rows[at : at + 1]
-            return near[slot[side], at : at + 1, :]
+                return lat[which, at : at + 1, :]
+            return near[slot[side], which, at : at + 1, :]
         wide[h + halo, inside] = upright(line((up, 0)))
         wide[h + halo, 0:PAD] = upright(line((up, -1)))[tile_cols - PAD :]
         wide[h + halo, PAD + tile_cols :] = upright(line((up, 1)))[:PAD]
-
-    def product(source, q):
-        x = held[pl.ds(pl.multiple_of(source * group, group), group), q * GROUP : (q + 1) * GROUP, :]
-        x = jnp.transpose(jnp.swapaxes(x, 0, 1), (0, 2, 1)).reshape(GROUP * tile_cols, group)
+        gain[h + halo] = upright(line((up, 0), 1))
+
+    def frames_of(source):
+        return pl.ds(pl.multiple_of(source * group, group), group)
+
+    def product(x, source):
+        count = x.shape[0]
+        x = jnp.transpose(x, (0, 2, 1)).reshape(count * tile_cols, group)
         high = x.astype(jnp.bfloat16)
         low = (x - high.astype(jnp.float32)).astype(jnp.bfloat16)
-        at = pl.ds(pl.multiple_of(source * group, group), group)
+        at = frames_of(source)
         out = jnp.dot(high, mix_ref[0, at], preferred_element_type=jnp.float32)
         out += jnp.dot(low, mix_ref[0, at], preferred_element_type=jnp.float32)
         out += jnp.dot(high, mix_ref[1, at], preferred_element_type=jnp.float32)
-        return out.reshape(GROUP, tile_cols, total)
-
-    def part(q):
-        return slice(halo + q * GROUP, halo + (q + 1) * GROUP)
-
-    def arrived(k):
+        return out.reshape(count, tile_cols, total)
+
+    def wait_for(ref, sem):
+        pltpu.make_async_copy(ref, ref, sem).wait()
+
+    def relayed(side, at_row, source):
+        if side == 0:
+            return (at_row >= 1) & jnp.logical_not((at_row == mid) & (source < mid))
+        return (at_row < rows - 1) & jnp.logical_not((at_row == mid - 1) & (source >= mid))
+
+    def relay_copy(side, k):
+        source = lax.rem(row - k + rows, rows)
+        at = frames_of(source)
+        return pltpu.make_async_remote_copy(
+            src_ref=edge.at[side, :, at], dst_ref=rim.at[1 - side, :, at],
+            send_sem=relay_send.at[side, k], recv_sem=relay_recv.at[1 - side, k],
+            device_id=(row + (1 if side else -1), col), device_id_type=MESH,
+        )
+
+    def full(value):
+        return jnp.concatenate([value] * (total // LANES), axis=-1)
+
+    last = tile_rows // GROUP - 1
+
+    def main_part(k, finish):
+        source = lax.rem(row - k + rows, rows)
         if k == 0:
             own.wait()
-            blocks = held.at[pl.ds(0, group - local)]
+            wait_for(held.at[pl.ds(0, group - local)], recv_sem.at[k])
         else:
-            blocks = held.at[pl.ds(0, group)]
-        pltpu.make_async_copy(blocks, blocks, recv_sem.at[k]).wait()
-        return lax.rem(row - k + rows, rows)
+            wait_for(held.at[pl.ds(0, group)], recv_sem.at[k])
+        at = frames_of(source)
+        for q in range(last + 1):
+            x = jnp.swapaxes(held[at, q * GROUP : (q + 1) * GROUP, :], 0, 1)
+            if q == 0:
+                edge[0, :, at] = x[:halo]
+            if q == last:
+                edge[1, :, at] = x[GROUP - halo :]
+        for side in range(2):
+            @pl.when(relayed(side, row, source))
+            def _(side=side):
+                relay_copy(side, k).start()
+        for q in range(last + 1):
+            x = jnp.swapaxes(held[at, q * GROUP : (q + 1) * GROUP, :], 0, 1)
+            here = slice(halo + q * GROUP, halo + (q + 1) * GROUP)
+            value = flux[here, inside] + product(x, source)
+            flux[here, inside] = value * full(gain[here]) if finish else value
+
+    def halo_part(k, finish):
+        for side in range(2):
+            beyond = row + (1 if side else -1)
+            source = lax.rem(beyond - k + rows, rows)
+            at = frames_of(source)
+            here = slice(halo + tile_rows, 2 * halo + tile_rows) if side else slice(0, halo)
+
+            @pl.when(there(1 if side else -1, rows, row))
+            def _(side=side, beyond=beyond, source=source, at=at, here=here):
+                direct = jnp.logical_not(relayed(1 - side, beyond, source))
+
+                @pl.when(direct)
+                def _():
+                    turn = source - half * mid
+
+                    @pl.when(source == row)
+                    def _():
+                        strip_self.wait()
+                        wait_for(strip.at[pl.ds(0, group - local)], strip_recv.at[turn])
+
+                    @pl.when(source != row)
+                    def _():
+                        wait_for(strip.at[pl.ds(0, group)], strip_recv.at[turn])
+
+                    x = jnp.swapaxes(strip[frames_of(turn)], 0, 1)
+                    rim[side, :, at] = x[:halo] if side else x[GROUP - halo :]
+
+                @pl.when(jnp.logical_not(direct))
+                def _():
+                    wait_for(rim.at[side, :, at], relay_recv.at[side, k])
+
+                value = flux[here, inside] + product(rim[side, :, at], source)
+                flux[here, inside] = value * full(gain[here]) if finish else value
 
     visits = [k for k in order if k]
     visits = visits[:-1] + [0] + visits[-1:]
     for k in visits[:-1]:
-        source = arrived(k)
-        for q in range(tile_rows // GROUP):
-            flux[part(q), inside] += product(source, q)
-
-    col_spans = {-1: (PAD, PAD + tile_cols), 1: (tile_cols, 0)}
-
-    def halo_copy(i):
-        up, aside = SIDES[i]
-        near_rows = halo if aside == 0 else halo - 1
-        if up == 0:
-            from_rows = to_rows = pl.ds(halo, tile_rows)
-        elif up < 0:
-            from_rows, to_rows = pl.ds(halo, near_rows), pl.ds(halo + tile_rows, near_rows)
-        else:
-            from_rows = pl.ds(halo + tile_rows - near_rows, near_rows)
-            to_rows = pl.ds(halo - near_rows, near_rows)
-        if aside == 0:
-            from_cols = to_cols = pl.ds(PAD, tile_cols)
-        else:
-            from_cols = pl.ds(col_spans[aside][0], PAD)
-            to_cols = pl.ds(col_spans[aside][1], PAD)
+        main_part(k, False)
+    for k in visits[:-2]:
+        halo_part(k, False)
+    main_part(visits[-1], True)
+    halo_part(visits[-2], False)
+    halo_part(visits[-1], True)
+
+    def side_copy(i):
         return pltpu.make_async_remote_copy(
-            src_ref=flux.at[from_rows, from_cols], dst_ref=flux.at[to_rows, to_cols],
-            send_sem=halo_send.at[i], recv_sem=halo_recv.at[i],
-            device_id=(row + up, col + aside), device_id_type=MESH,
+            src_ref=side_out.at[i], dst_ref=side_in.at[1 - i],
+            send_sem=side_send.at[i], recv_sem=side_recv.at[1 - i],
+            device_id=(row, col + (1 if i else -1)), device_id_type=MESH,
         )
 
-    def send_halo(i):
-        @pl.when(exists(SIDES[i]))
-        def _():
-            halo_copy(i).start()
-
-    source = arrived(visits[-1])
-    last = tile_rows // GROUP - 1
-    for q in range(last + 1):
-        here = slice(q * GROUP, (q + 1) * GROUP)
-        g = jnp.concatenate([gain[here]] * (total // LANES), axis=-1)
-        flux[part(q), inside] = (flux[part(q), inside] + product(source, q)) * g
-        for i, side in enumerate(SIDES):
-            if (side[0] == -1 and q == 0) or (side[0] == 1 and q == last):
-                send_halo(i)
-    for i, side in enumerate(SIDES):
-        if side[0] == 0:
-            send_halo(i)
-
-    sent = held.at[pl.ds(0, total - local)]
-    pltpu.make_async_copy(sent, sent, send_sem).wait()
-    for i, side in enumerate(SIDES):
-        @pl.when(exists(side))
+    for i in range(2):
+        for j in range(halo):
+            at = PAD + j + (tile_cols - halo if i else 0)
+            side_out[i, j] = flux[:, at, :]
+    for i in range(2):
+        @pl.when(there(1 if i else -1, cols, col))
         def _(i=i):
-            halo_copy(i).wait_send()
-        @pl.when(exists((-side[0], -side[1])))
+            side_copy(i).start()
+
+    wait_for(held.at[pl.ds(0, total - local)], send_sem)
+
+    @pl.when(beside)
+    def _():
+        wait_for(strip.at[pl.ds(0, group - local)], strip_send)
+
+    @pl.when(jnp.logical_not(beside))
+    def _():
+        wait_for(strip.at[pl.ds(0, group)], strip_send)
+
+    for k in range(rows):
+        for side in range(2):
+            @pl.when(relayed(side, row, lax.rem(row - k + rows, rows)))
+            def _(side=side, k=k):
+                relay_copy(side, k).wait_send()
+    for i in range(2):
+        @pl.when(there(1 if i else -1, cols, col))
         def _(i=i):
-            halo_copy(i).wait_recv()
+            side_copy(i).wait_send()
+            wait_for(side_in.at[i], side_recv.at[i])
+            for j in range(halo):
+                at = PAD + tile_cols + j if i else PAD - halo + j
+                flux[:, at, :] = side_in[i, j]
 
 
 def relax_kernel(flux, wide, out, first, second):
@@ -316,7 +405,7 @@
     local, height, width = frames.shape
     tile_rows, tile_cols = height // rows, width // cols
     total = local * rows * cols
-    if local % 8 or tile_rows % GROUP or tile_cols != LANES or total % LANES or (local * cols) % LANES:
+    if rows % 2 or local % 8 or tile_rows % GROUP or tile_cols != LANES or total % LANES or (local * cols) % LANES:
         return plain_device(frames, class_index, surface_mask, effusivity, conductivity)
     high_rows, wide_cols = tile_rows + 2 * PASSES, tile_cols + 2 * PAD
     vmem = pl.BlockSpec(memory_space=pltpu.VMEM)
@@ -333,11 +422,17 @@
         out_specs=(vmem, vmem),
         scratch_shapes=[
             pltpu.VMEM((total, tile_rows, tile_cols), jnp.float32),
-            pltpu.VMEM((tile_rows, tile_cols), jnp.float32),
-            pltpu.VMEM((sides, tile_rows, tile_cols), jnp.float32),
-            pltpu.VMEM((tile_rows, tile_cols, LANES), jnp.float32),
+            pltpu.VMEM((2, tile_rows, tile_cols), jnp.float32),
+            pltpu.VMEM((sides, 2, tile_rows, tile_cols), jnp.float32),
+            pltpu.VMEM((high_rows, tile_cols, LANES), jnp.float32),
             pltpu.VMEM((2, total, total), jnp.bfloat16),
-            dma, dma((rows,)), dma, dma((sides,)), dma((sides,)), dma((sides,)), dma((sides,)),
+            pltpu.VMEM((2, PASSES, total, tile_cols), jnp.float32),
+            pltpu.VMEM((2, PASSES, total, tile_cols), jnp.float32),
+            pltpu.VMEM((total // 2, GROUP, tile_cols), jnp.float32),
+            pltpu.VMEM((2, PASSES, high_rows, total), jnp.float32),
+            pltpu.VMEM((2, PASSES, high_rows, total), jnp.float32),
+            dma, dma((rows,)), dma, dma((sides,)), dma((sides,)),
+            dma, dma((rows // 2,)), dma, dma((2, rows)), dma((2, rows)), dma((2,)), dma((2,)),
         ],
         compiler_params=pltpu.CompilerParams(
             collective_id=0, has_side_effects=True, vmem_limit_bytes=40 * 2**20

time: 135 us -> 129 us (0.956)
  Pallas kernels: 128 us -> 122 us
    pallas_call x1, Pallas kernels: 122 us -> 116 us  [per_device(): pl.pallas_call(functools.partial(gather_kernel, rows, cols, tile_rows, ti...]
where the time goes in v2:
time: 129 us; the launch traced here: 127 us
  Pallas kernels  122 us (95%)
  local copies, waits for them, and re-layouts  4.89 us (4%)
    pallas_call x1, Pallas kernels, per_device(): pl.pallas_call(functools.partial(gather_kernel, rows, cols, tile_rows, ti...  116 us
    pallas_call x1, Pallas kernels, per_device(): pl.pallas_call(relax_kernel, out_shape=jax.ShapeDtypeStruct((tile_rows, t...  6.42 us
    unnamed x10, local copies, waits for them, and re-layouts  4.89 us

profile of v2, /device:TPU:19, one launch (start us, length us, event | category | flops | bytes accessed | tf_op | source)
XLA Modules:
  0.0 127.2 jit_solution(12407222621991920899)
XLA Ops:
  0.0 0.0 copy-start
  0.0 2.2 %copy-done = f32[16,64,1024]{2,1,0:T(8,128)S(1)} copy-done((f32[16,64,1024]{2,1,0:T(8,128)S(1)}, f32[16,64,1024]{2,1,0:T(8,128)}, u32[]{:S(2)}) %copy-start) | copy-done | bytes 4194328
  2.2 0.0 copy-start.1
  2.2 0.7 copy-done.1
  2.9 0.0 copy-start.2
  2.9 0.7 copy-done.2
  3.6 0.0 copy-start.3
  3.6 0.7 copy-done.3
  4.2 0.0 copy-start.4
  4.2 0.7 copy-done.4
  4.9 115.8 %gather.1 = (f32[22,144,512]{2,1,0:T(8,128)S(1)}, f32[22,144,128]{2,1,0:T(8,128)S(1)}) custom-call(f32[16,64,1024]{2,1,0:T(8,128)S(1)} %copy-done, s32[16,128]{1,0:T(8,128)S(1)} %copy-done.1, s32[16,128]{1,0:T(8,128)S(1)} %copy-done.2, f32[8]{0:T(128)S(1)} %copy-done.3, f32[8]{0:T(128)S(1)} %copy-done.4), custom_call_target="tpu_custom_call" | custom-call | tf_op jit(solution)/shard_map/gather/pallas_call | solution.py:415
  120.7 6.4 %relax.1 = f32[16,128,512]{2,1,0:T(8,128)} custom-call(f32[22,144,512]{2,1,0:T(8,128)S(1)} %get-tuple-element.7.flux, f32[22,144,128]{2,1,0:T(8,128)S(1)} %get-tuple-element.8.wide), custom_call_target="tpu_custom_call" | custom-call | tf_op jit(solution)/shard_map/relax/pallas_call | solution.py:442
Async XLA Ops:
  0.0 2.2 %copy-start = (f32[16,64,1024]{2,1,0:T(8,128)S(1)}, f32[16,64,1024]{2,1,0:T(8,128)}, u32[]{:S(2)}) copy-start(f32[16,64,1024]{2,1,0:T(8,128)} %frames.1) | copy-start | bytes 12582916
  2.2 0.7 copy-start.1
  2.9 0.7 copy-start.2
  3.6 0.7 copy-start.3
  4.2 0.7 copy-start.4

commit v3 on v2

--- a/solution.py
+++ b/solution.py
@@ -10,6 +10,7 @@
 PAD = 8
 GROUP = 8
 LANES = 128
+VMEM_GATHER = 40 * 2**20
 MESH = pl.DeviceIdType.MESH
 
 flux_factor = 1.1283791670955126
@@ -100,6 +101,7 @@
     group = cols * local
     total = rows * group
     halo = PASSES
+    chunks = total // LANES
     mid = rows // 2
     half = row // mid
 
@@ -124,7 +126,8 @@
 
     @pl.loop(0, tile_rows + 2 * halo)
     def _(h):
-        flux[h] = jnp.zeros(flux.shape[1:], jnp.float32)
+        for c in range(chunks):
+            flux[c, h] = jnp.zeros(flux.shape[2:], jnp.float32)
 
     barrier = pltpu.get_barrier_semaphore()
     for k in range(rows):
@@ -147,7 +150,42 @@
     def column(at):
         return pl.ds(pl.multiple_of(at * tile_cols, tile_cols), tile_cols)
 
-    order = [rows // 2] + [k for k in range(rows) if k != rows // 2 and k] + [0]
+    own = pltpu.make_async_copy(
+        frames.at[:, pl.ds(pl.multiple_of(row * tile_rows, tile_rows), tile_rows), column(col)],
+        held.at[pl.ds((row * cols + col) * local, local)],
+        own_sem,
+    )
+    own.start()
+
+    strip_row = mid - 1 + half
+    strip_from = pl.ds(pl.multiple_of(mid * tile_rows - GROUP * half, GROUP), GROUP)
+    strip_at = strip.at[pl.ds(((row - half * mid) * cols + col) * local, local)]
+    beside = row == strip_row
+
+    def strip_copy(j):
+        to_col = lax.rem(col + j, cols)
+        return pltpu.make_async_remote_copy(
+            src_ref=frames.at[:, strip_from, column(to_col)], dst_ref=strip_at,
+            send_sem=strip_send, recv_sem=strip_recv.at[row - half * mid],
+            device_id=(strip_row, to_col), device_id_type=MESH,
+        )
+
+    strip_self = pltpu.make_async_copy(frames.at[:, strip_from, column(col)], strip_at, strip_own)
+
+    def start_strips():
+        @pl.loop(1, cols)
+        def _(j):
+            strip_copy(j).start()
+
+        @pl.when(beside)
+        def _():
+            strip_self.start()
+
+        @pl.when(jnp.logical_not(beside))
+        def _():
+            strip_copy(0).start()
+
+    order = [2, 0, 1, 3]
     for k in order:
         @pl.loop(0 if k else 1, cols)
         def _(j, k=k):
@@ -160,45 +198,13 @@
                 send_sem=send_sem, recv_sem=recv_sem.at[k],
                 device_id=(to_row, to_col), device_id_type=MESH,
             ).start()
+        if k == 0:
+            start_strips()
         if k == order[0]:
             for i, side in enumerate(SIDES):
                 @pl.when(exists(side))
                 def _(i=i):
                     lat_copy(i).start()
-    own = pltpu.make_async_copy(
-        frames.at[:, pl.ds(pl.multiple_of(row * tile_rows, tile_rows), tile_rows), column(col)],
-        held.at[pl.ds((row * cols + col) * local, local)],
-        own_sem,
-    )
-    own.start()
-
-    strip_row = mid - 1 + half
-    strip_from = pl.ds(pl.multiple_of(mid * tile_rows - GROUP * half, GROUP), GROUP)
-    strip_at = strip.at[pl.ds(((row - half * mid) * cols + col) * local, local)]
-    beside = row == strip_row
-
-    def strip_copy(j):
-        to_col = lax.rem(col + j, cols)
-        return pltpu.make_async_remote_copy(
-            src_ref=frames.at[:, strip_from, column(to_col)], dst_ref=strip_at,
-            send_sem=strip_send, recv_sem=strip_recv.at[row - half * mid],
-            device_id=(strip_row, to_col), device_id_type=MESH,
-        )
-
-    @pl.loop(1, cols)
-    def _(j):
-        strip_copy(j).start()
-
-    strip_self = pltpu.make_async_copy(frames.at[:, strip_from, column(col)], strip_at, strip_own)
-
-    @pl.when(beside)
-    def _():
-        strip_self.start()
-
-    @pl.when(jnp.logical_not(beside))
-    def _():
-        strip_copy(0).start()
-
     for k in range(rows):
         shape = (group, total)
         earlier = lax.broadcasted_iota(jnp.int32, shape, 0) + k * group
@@ -264,8 +270,10 @@
             device_id=(row + (1 if side else -1), col), device_id_type=MESH,
         )
 
-    def full(value):
-        return jnp.concatenate([value] * (total // LANES), axis=-1)
+    def add(here, out, finish):
+        for c in range(chunks):
+            value = flux[c, here, inside] + out[:, :, c * LANES : (c + 1) * LANES]
+            flux[c, here, inside] = value * gain[here] if finish else value
 
     last = tile_rows // GROUP - 1
 
@@ -290,8 +298,7 @@
         for q in range(last + 1):
             x = jnp.swapaxes(held[at, q * GROUP : (q + 1) * GROUP, :], 0, 1)
             here = slice(halo + q * GROUP, halo + (q + 1) * GROUP)
-            value = flux[here, inside] + product(x, source)
-            flux[here, inside] = value * full(gain[here]) if finish else value
+            add(here, product(x, source), finish)
 
     def halo_part(k, finish):
         for side in range(2):
@@ -324,11 +331,9 @@
                 def _():
                     wait_for(rim.at[side, :, at], relay_recv.at[side, k])
 
-                value = flux[here, inside] + product(rim[side, :, at], source)
-                flux[here, inside] = value * full(gain[here]) if finish else value
-
-    visits = [k for k in order if k]
-    visits = visits[:-1] + [0] + visits[-1:]
+                add(here, product(rim[side, :, at], source), finish)
+
+    visits = [2, 0, 1, 3]
     for k in visits[:-1]:
         main_part(k, False)
     for k in visits[:-2]:
@@ -347,7 +352,8 @@
     for i in range(2):
         for j in range(halo):
             at = PAD + j + (tile_cols - halo if i else 0)
-            side_out[i, j] = flux[:, at, :]
+            for c in range(chunks):
+                side_out[i, j, c] = flux[c, :, at, :]
     for i in range(2):
         @pl.when(there(1 if i else -1, cols, col))
         def _(i=i):
@@ -375,28 +381,37 @@
             wait_for(side_in.at[i], side_recv.at[i])
             for j in range(halo):
                 at = PAD + tile_cols + j if i else PAD - halo + j
-                flux[:, at, :] = side_in[i, j]
-
-
-def relax_kernel(flux, wide, out, first, second):
-    source = flux
-    count, width = flux.shape[0], flux.shape[1]
-    for step, target in enumerate((first, second, out)):
-        low, high = step + 1, count - step - 1
-        edge = (1 + step, width - 1 - step) if target is not out else (PAD, width - PAD)
-        for h in range(low, high):
-            a, b = edge
-            center = source[h, a:b, :]
-            laplace = (
-                source[h + 1, a:b, :] + source[h - 1, a:b, :]
-                + source[h, a + 1 : b + 1, :] + source[h, a - 1 : b - 1, :] - 4.0 * center
-            )
-            value = center + wide[h, a:b, :] * laplace
-            if target is out:
-                out[h - PASSES] = value
-            else:
-                target[h, a:b, :] = value
-        source = target
+                for c in range(chunks):
+                    flux[c, :, at, :] = side_in[i, j, c]
+
+
+def relax_kernel(flux, wide, out, first, second, third, sem):
+    chunks, count, width = flux.shape[0], flux.shape[1], flux.shape[2]
+
+    def out_copy(c):
+        return pltpu.make_async_copy(
+            third.at[c], out.at[:, :, c * LANES : (c + 1) * LANES], sem.at[c]
+        )
+
+    for c in range(chunks):
+        source = flux.at[c]
+        for step, target in enumerate((first, second, None)):
+            a, b = (1 + step, width - 1 - step) if target is not None else (PAD, width - PAD)
+            for h in range(step + 1, count - step - 1):
+                center = source[h, a:b, :]
+                laplace = (
+                    source[h + 1, a:b, :] + source[h - 1, a:b, :]
+                    + source[h, a + 1 : b + 1, :] + source[h, a - 1 : b - 1, :] - 4.0 * center
+                )
+                value = center + wide[h, a:b, :] * laplace
+                if target is None:
+                    third[c, h - PASSES] = value
+                else:
+                    target[h, a:b, :] = value
+            source = target
+        out_copy(c).start()
+    for c in range(chunks):
+        out_copy(c).wait()
 
 
 def per_device(frames, class_index, surface_mask, effusivity, conductivity):
@@ -407,15 +422,17 @@
     total = local * rows * cols
     if rows % 2 or local % 8 or tile_rows % GROUP or tile_cols != LANES or total % LANES or (local * cols) % LANES:
         return plain_device(frames, class_index, surface_mask, effusivity, conductivity)
+    chunks = total // LANES
     high_rows, wide_cols = tile_rows + 2 * PASSES, tile_cols + 2 * PAD
     vmem = pl.BlockSpec(memory_space=pltpu.VMEM)
     smem = pl.BlockSpec(memory_space=pltpu.SMEM)
     dma = pltpu.SemaphoreType.DMA
     sides = len(SIDES)
+    arguments = (frames, class_index, surface_mask, effusivity, conductivity)
     flux, wide = pl.pallas_call(
         functools.partial(gather_kernel, rows, cols, tile_rows, tile_cols, local),
         out_shape=(
-            jax.ShapeDtypeStruct((high_rows, wide_cols, total), jnp.float32),
+            jax.ShapeDtypeStruct((chunks, high_rows, wide_cols, LANES), jnp.float32),
             jax.ShapeDtypeStruct((high_rows, wide_cols, LANES), jnp.float32),
         ),
         in_specs=[pl.BlockSpec(memory_space=pltpu.HBM), vmem, vmem, smem, smem],
@@ -429,26 +446,23 @@
             pltpu.VMEM((2, PASSES, total, tile_cols), jnp.float32),
             pltpu.VMEM((2, PASSES, total, tile_cols), jnp.float32),
             pltpu.VMEM((total // 2, GROUP, tile_cols), jnp.float32),
-            pltpu.VMEM((2, PASSES, high_rows, total), jnp.float32),
-            pltpu.VMEM((2, PASSES, high_rows, total), jnp.float32),
+            pltpu.VMEM((2, PASSES, chunks, high_rows, LANES), jnp.float32),
+            pltpu.VMEM((2, PASSES, chunks, high_rows, LANES), jnp.float32),
             dma, dma((rows,)), dma, dma((sides,)), dma((sides,)),
             dma, dma((rows // 2,)), dma, dma((2, rows)), dma((2, rows)), dma((2,)), dma((2,)),
         ],
         compiler_params=pltpu.CompilerParams(
-            collective_id=0, has_side_effects=True, vmem_limit_bytes=40 * 2**20
+            collective_id=0, has_side_effects=True, vmem_limit_bytes=VMEM_GATHER
         ),
         name="gather",
-    )(frames, class_index, surface_mask, effusivity, conductivity)
+    )(*(pltpu.with_memory_space_constraint(x, pltpu.HBM) for x in arguments))
     return pl.pallas_call(
         relax_kernel,
         out_shape=jax.ShapeDtypeStruct((tile_rows, tile_cols, total), jnp.float32),
-        grid=(total // LANES,),
-        in_specs=[
-            pl.BlockSpec((high_rows, wide_cols, LANES), lambda n: (0, 0, n)),
-            pl.BlockSpec((high_rows, wide_cols, LANES), lambda n: (0, 0, 0)),
-        ],
-        out_specs=pl.BlockSpec((tile_rows, tile_cols, LANES), lambda n: (0, 0, n)),
-        scratch_shapes=[pltpu.VMEM((high_rows, wide_cols, LANES), jnp.float32)] * 2,
+        in_specs=[vmem, vmem],
+        out_specs=pl.BlockSpec(memory_space=pltpu.HBM),
+        scratch_shapes=[pltpu.VMEM((high_rows, wide_cols, LANES), jnp.float32)] * 2
+        + [pltpu.VMEM((chunks, tile_rows, tile_cols, LANES), jnp.float32), dma((chunks,))],
         compiler_params=pltpu.CompilerParams(vmem_limit_bytes=24 * 2**20),
         name="relax",
     )(flux, wide)

time: 129 us -> 122 us (0.946)
  local copies, waits for them, and re-layouts: 4.89 us -> 0 us
  Pallas kernels: 122 us -> 119 us
    unnamed x10 -> x0, local copies, waits for them, and re-layouts: 4.89 us -> none
    pallas_call x1, Pallas kernels: 116 us -> 114 us  [per_device(): pl.pallas_call(functools.partial(gather_kernel, rows, cols, tile_rows, ti...]
where the time goes in v3:
time: 122 us; the launch traced here: 119 us
  Pallas kernels  119 us (98%)
    pallas_call x1, Pallas kernels, per_device(): pl.pallas_call(functools.partial(gather_kernel, rows, cols, tile_rows, ti...  114 us
    pallas_call x1, Pallas kernels, per_device(): pl.pallas_call(relax_kernel, out_shape=jax.ShapeDtypeStruct((tile_rows, t...  5.28 us

profile of v3, /device:TPU:19, one launch (start us, length us, event | category | flops | bytes accessed | tf_op | source)
XLA Modules:
  0.0 119.3 jit_solution(5354879022469061208)
XLA Ops:
  0.0 113.8 %gather.1 = (f32[4,22,144,128]{3,2,1,0:T(8,128)S(1)}, f32[22,144,128]{2,1,0:T(8,128)S(1)}) custom-call(f32[16,64,1024]{2,1,0:T(8,128)} %frames.1, s32[16,128]{1,0:T(8,128)} %class_ref.1, s32[16,128]{1,0:T(8,128)} %mask_ref.1, f32[8]{0:T(128)} %eff_ref.1, f32[8]{0:T(128)} %cond_ref.1), custom_call_target="tpu_custom_call" | custom-call | tf_op jit(solution)/shard_map/gather/pallas_call | solution.py:432
  113.8 5.3 %relax.1 = f32[16,128,512]{2,1,0:T(8,128)} custom-call(f32[4,22,144,128]{3,2,1,0:T(8,128)S(1)} %get-tuple-element.7.flux, f32[22,144,128]{2,1,0:T(8,128)S(1)} %get-tuple-element.8.wide), custom_call_target="tpu_custom_call" | custom-call | tf_op jit(solution)/shard_map/relax/pallas_call | solution.py:459

commit v4 on v3

--- a/solution.py
+++ b/solution.py
@@ -185,7 +185,7 @@
         def _():
             strip_copy(0).start()
 
-    order = [2, 0, 1, 3]
+    order = [mid, 0] + [k for k in range(1, rows) if k != mid]
     for k in order:
         @pl.loop(0 if k else 1, cols)
         def _(j, k=k):
@@ -333,7 +333,7 @@
 
                 add(here, product(rim[side, :, at], source), finish)
 
-    visits = [2, 0, 1, 3]
+    visits = order
     for k in visits[:-1]:
         main_part(k, False)
     for k in visits[:-2]:
@@ -396,18 +396,24 @@
     for c in range(chunks):
         source = flux.at[c]
         for step, target in enumerate((first, second, None)):
-            a, b = (1 + step, width - 1 - step) if target is not None else (PAD, width - PAD)
-            for h in range(step + 1, count - step - 1):
-                center = source[h, a:b, :]
-                laplace = (
-                    source[h + 1, a:b, :] + source[h - 1, a:b, :]
-                    + source[h, a + 1 : b + 1, :] + source[h, a - 1 : b - 1, :] - 4.0 * center
-                )
-                value = center + wide[h, a:b, :] * laplace
-                if target is None:
-                    third[c, h - PASSES] = value
-                else:
-                    target[h, a:b, :] = value
+            if target is None:
+                bounds = [PAD, PAD + (width - 2 * PAD) // 2, width - PAD]
+            else:
+                bounds = [1 + step, width // 2, width - 1 - step]
+            for a, b in zip(bounds[:-1], bounds[1:]):
+                above, center = source[step, a:b, :], source[step + 1, a:b, :]
+                for h in range(step + 1, count - step - 1):
+                    below = source[h + 1, a:b, :]
+                    laplace = (
+                        below + above
+                        + source[h, a + 1 : b + 1, :] + source[h, a - 1 : b - 1, :] - 4.0 * center
+                    )
+                    value = center + wide[h, a:b, :] * laplace
+                    if target is None:
+                        third[c, h - PASSES, a - PAD : b - PAD] = value
+                    else:
+                        target[h, a:b, :] = value
+                    above, center = center, below
             source = target
         out_copy(c).start()
     for c in range(chunks):

time: 122 us -> 121 us (level)
  no operation moved by 1% of the time
where the time goes in v4:
time: 121 us; the launch traced here: 119 us
  Pallas kernels  118 us (98%)
    pallas_call x1, Pallas kernels, per_device(): pl.pallas_call(functools.partial(gather_kernel, rows, cols, tile_rows, ti...  114 us
    pallas_call x1, Pallas kernels, per_device(): pl.pallas_call(relax_kernel, out_shape=jax.ShapeDtypeStruct((tile_rows, t...  4.57 us

profile of v4, /device:TPU:19, one launch (start us, length us, event | category | flops | bytes accessed | tf_op | source)
XLA Modules:
  0.0 118.6 jit_solution(17021822981523047896)
XLA Ops:
  0.0 113.8 %gather.1 = (f32[4,22,144,128]{3,2,1,0:T(8,128)S(1)}, f32[22,144,128]{2,1,0:T(8,128)S(1)}) custom-call(f32[16,64,1024]{2,1,0:T(8,128)} %frames.1, s32[16,128]{1,0:T(8,128)} %class_ref.1, s32[16,128]{1,0:T(8,128)} %mask_ref.1, f32[8]{0:T(128)} %eff_ref.1, f32[8]{0:T(128)} %cond_ref.1), custom_call_target="tpu_custom_call" | custom-call | tf_op jit(solution)/shard_map/gather/pallas_call | solution.py:438
  113.8 4.6 %relax.1 = f32[16,128,512]{2,1,0:T(8,128)} custom-call(f32[4,22,144,128]{3,2,1,0:T(8,128)S(1)} %get-tuple-element.7.flux, f32[22,144,128]{2,1,0:T(8,128)S(1)} %get-tuple-element.8.wide), custom_call_target="tpu_custom_call" | custom-call | tf_op jit(solution)/shard_map/relax/pallas_call | solution.py:465

commit v5 on v4

--- a/solution.py
+++ b/solution.py
@@ -186,18 +186,33 @@
             strip_copy(0).start()
 
     order = [mid, 0] + [k for k in range(1, rows) if k != mid]
+    final = order[-1]
+    part_cols = cols // 2
+    part = group // 2
+    own_part = col // part_cols
+
+    def send(k, to_col, sem):
+        to_row = lax.rem(row + k, rows)
+        pltpu.make_async_remote_copy(
+            src_ref=frames.at[
+                :, pl.ds(pl.multiple_of(to_row * tile_rows, tile_rows), tile_rows), column(to_col)
+            ],
+            dst_ref=held.at[pl.ds((row * cols + col) * local, local)],
+            send_sem=send_sem, recv_sem=recv_sem.at[sem],
+            device_id=(to_row, to_col), device_id_type=MESH,
+        ).start()
+
     for k in order:
-        @pl.loop(0 if k else 1, cols)
-        def _(j, k=k):
-            to_row, to_col = lax.rem(row + k, rows), lax.rem(col + j, cols)
-            pltpu.make_async_remote_copy(
-                src_ref=frames.at[
-                    :, pl.ds(pl.multiple_of(to_row * tile_rows, tile_rows), tile_rows), column(to_col)
-                ],
-                dst_ref=held.at[pl.ds((row * cols + col) * local, local)],
-                send_sem=send_sem, recv_sem=recv_sem.at[k],
-                device_id=(to_row, to_col), device_id_type=MESH,
-            ).start()
+        if k and k == final:
+            for turn in range(2):
+                @pl.loop(0, part_cols)
+                def _(j, k=k, turn=turn):
+                    half_at = lax.rem(own_part + turn, 2) * part_cols
+                    send(k, half_at + lax.rem(col + j, part_cols), rows if turn else k)
+        else:
+            @pl.loop(0 if k else 1, cols)
+            def _(j, k=k):
+                send(k, lax.rem(col + j, cols), k)
         if k == 0:
             start_strips()
         if k == order[0]:
@@ -242,12 +257,17 @@
     def frames_of(source):
         return pl.ds(pl.multiple_of(source * group, group), group)
 
-    def product(x, source):
+    def piece(source, turn):
+        if turn is None:
+            return frames_of(source)
+        which = lax.rem(own_part + turn, 2)
+        return pl.ds(pl.multiple_of(source * group + which * part, part), part)
+
+    def product(x, at):
         count = x.shape[0]
-        x = jnp.transpose(x, (0, 2, 1)).reshape(count * tile_cols, group)
+        x = jnp.transpose(x, (0, 2, 1)).reshape(count * tile_cols, x.shape[1])
         high = x.astype(jnp.bfloat16)
         low = (x - high.astype(jnp.float32)).astype(jnp.bfloat16)
-        at = frames_of(source)
         out = jnp.dot(high, mix_ref[0, at], preferred_element_type=jnp.float32)
         out += jnp.dot(low, mix_ref[0, at], preferred_element_type=jnp.float32)
         out += jnp.dot(high, mix_ref[1, at], preferred_element_type=jnp.float32)
@@ -261,9 +281,10 @@
             return (at_row >= 1) & jnp.logical_not((at_row == mid) & (source < mid))
         return (at_row < rows - 1) & jnp.logical_not((at_row == mid - 1) & (source >= mid))
 
-    def relay_copy(side, k):
+    def relay_copy(side, k, turn=None):
         source = lax.rem(row - k + rows, rows)
-        at = frames_of(source)
+        at = piece(source, turn)
+        k = rows if turn else k
         return pltpu.make_async_remote_copy(
             src_ref=edge.at[side, :, at], dst_ref=rim.at[1 - side, :, at],
             send_sem=relay_send.at[side, k], recv_sem=relay_recv.at[1 - side, k],
@@ -277,14 +298,15 @@
 
     last = tile_rows // GROUP - 1
 
-    def main_part(k, finish):
+    def main_part(k, finish, turn=None):
         source = lax.rem(row - k + rows, rows)
         if k == 0:
             own.wait()
             wait_for(held.at[pl.ds(0, group - local)], recv_sem.at[k])
         else:
-            wait_for(held.at[pl.ds(0, group)], recv_sem.at[k])
-        at = frames_of(source)
+            size = group if turn is None else part
+            wait_for(held.at[pl.ds(0, size)], recv_sem.at[rows if turn else k])
+        at = piece(source, turn)
         for q in range(last + 1):
             x = jnp.swapaxes(held[at, q * GROUP : (q + 1) * GROUP, :], 0, 1)
             if q == 0:
@@ -294,53 +316,60 @@
         for side in range(2):
             @pl.when(relayed(side, row, source))
             def _(side=side):
-                relay_copy(side, k).start()
+                relay_copy(side, k, turn).start()
         for q in range(last + 1):
             x = jnp.swapaxes(held[at, q * GROUP : (q + 1) * GROUP, :], 0, 1)
             here = slice(halo + q * GROUP, halo + (q + 1) * GROUP)
-            add(here, product(x, source), finish)
-
-    def halo_part(k, finish):
+            add(here, product(x, at), finish)
+
+    def halo_part(k, finish, turn=None):
         for side in range(2):
             beyond = row + (1 if side else -1)
             source = lax.rem(beyond - k + rows, rows)
-            at = frames_of(source)
+            at = piece(source, turn)
             here = slice(halo + tile_rows, 2 * halo + tile_rows) if side else slice(0, halo)
 
             @pl.when(there(1 if side else -1, rows, row))
             def _(side=side, beyond=beyond, source=source, at=at, here=here):
                 direct = jnp.logical_not(relayed(1 - side, beyond, source))
 
-                @pl.when(direct)
+                @pl.when(direct & (not turn))
                 def _():
-                    turn = source - half * mid
+                    slot = source - half * mid
 
                     @pl.when(source == row)
                     def _():
                         strip_self.wait()
-                        wait_for(strip.at[pl.ds(0, group - local)], strip_recv.at[turn])
+                        wait_for(strip.at[pl.ds(0, group - local)], strip_recv.at[slot])
 
                     @pl.when(source != row)
                     def _():
-                        wait_for(strip.at[pl.ds(0, group)], strip_recv.at[turn])
-
-                    x = jnp.swapaxes(strip[frames_of(turn)], 0, 1)
-                    rim[side, :, at] = x[:halo] if side else x[GROUP - halo :]
+                        wait_for(strip.at[pl.ds(0, group)], strip_recv.at[slot])
+
+                    x = jnp.swapaxes(strip[frames_of(slot)], 0, 1)
+                    rim[side, :, frames_of(source)] = x[:halo] if side else x[GROUP - halo :]
 
                 @pl.when(jnp.logical_not(direct))
                 def _():
-                    wait_for(rim.at[side, :, at], relay_recv.at[side, k])
-
-                add(here, product(rim[side, :, at], source), finish)
+                    wait_for(rim.at[side, :, at], relay_recv.at[side, rows if turn else k])
+
+                add(here, product(rim[side, :, at], at), finish)
 
     visits = order
     for k in visits[:-1]:
         main_part(k, False)
     for k in visits[:-2]:
         halo_part(k, False)
-    main_part(visits[-1], True)
-    halo_part(visits[-2], False)
-    halo_part(visits[-1], True)
+    if final:
+        main_part(final, False, 0)
+        main_part(final, True, 1)
+        halo_part(visits[-2], False)
+        halo_part(final, False, 0)
+        halo_part(final, True, 1)
+    else:
+        main_part(final, True)
+        halo_part(visits[-2], False)
+        halo_part(final, True)
 
     def side_copy(i):
         return pltpu.make_async_remote_copy(
@@ -373,7 +402,8 @@
         for side in range(2):
             @pl.when(relayed(side, row, lax.rem(row - k + rows, rows)))
             def _(side=side, k=k):
-                relay_copy(side, k).wait_send()
+                for turn in (0, 1) if k and k == final else (None,):
+                    relay_copy(side, k, turn).wait_send()
     for i in range(2):
         @pl.when(there(1 if i else -1, cols, col))
         def _(i=i):
@@ -426,7 +456,7 @@
     local, height, width = frames.shape
     tile_rows, tile_cols = height // rows, width // cols
     total = local * rows * cols
-    if rows % 2 or local % 8 or tile_rows % GROUP or tile_cols != LANES or total % LANES or (local * cols) % LANES:
+    if rows % 2 or cols % 2 or local % 8 or tile_rows % GROUP or tile_cols != LANES or total % LANES or (local * cols) % LANES or local * cols % 32:
         return plain_device(frames, class_index, surface_mask, effusivity, conductivity)
     chunks = total // LANES
     high_rows, wide_cols = tile_rows + 2 * PASSES, tile_cols + 2 * PAD
@@ -454,8 +484,8 @@
             pltpu.VMEM((total // 2, GROUP, tile_cols), jnp.float32),
             pltpu.VMEM((2, PASSES, chunks, high_rows, LANES), jnp.float32),
             pltpu.VMEM((2, PASSES, chunks, high_rows, LANES), jnp.float32),
-            dma, dma((rows,)), dma, dma((sides,)), dma((sides,)),
-            dma, dma((rows // 2,)), dma, dma((2, rows)), dma((2, rows)), dma((2,)), dma((2,)),
+            dma, dma((rows + 1,)), dma, dma((sides,)), dma((sides,)),
+            dma, dma((rows // 2,)), dma, dma((2, rows + 1)), dma((2, rows + 1)), dma((2,)), dma((2,)),
         ],
         compiler_params=pltpu.CompilerParams(
             collective_id=0, has_side_effects=True, vmem_limit_bytes=VMEM_GATHER

time: 121 us -> 121 us (level); the launches traced: 119 us -> 121 us
  Pallas kernels: 118 us -> 120 us
    pallas_call x1, Pallas kernels: 114 us -> 116 us  [per_device(): pl.pallas_call(functools.partial(gather_kernel, rows, cols, tile_rows, ti...]
where the time goes in v5:
time: 121 us
  Pallas kernels  120 us (99%)
    pallas_call x1, Pallas kernels, per_device(): pl.pallas_call(functools.partial(gather_kernel, rows, cols, tile_rows, ti...  116 us
    pallas_call x1, Pallas kernels, per_device(): pl.pallas_call(relax_kernel, out_shape=jax.ShapeDtypeStruct((tile_rows, t...  4.57 us

profile of v5, /device:TPU:19, one launch (start us, length us, event | category | flops | bytes accessed | tf_op | source)
XLA Modules:
  0.0 120.6 jit_solution(16199946841588956034)
XLA Ops:
  0.0 115.8 %gather.1 = (f32[4,22,144,128]{3,2,1,0:T(8,128)S(1)}, f32[22,144,128]{2,1,0:T(8,128)S(1)}) custom-call(f32[16,64,1024]{2,1,0:T(8,128)} %frames.1, s32[16,128]{1,0:T(8,128)} %class_ref.1, s32[16,128]{1,0:T(8,128)} %mask_ref.1, f32[8]{0:T(128)} %eff_ref.1, f32[8]{0:T(128)} %cond_ref.1), custom_call_target="tpu_custom_call" | custom-call | tf_op jit(solution)/shard_map/gather/pallas_call | solution.py:468
  115.8 4.6 %relax.1 = f32[16,128,512]{2,1,0:T(8,128)} custom-call(f32[4,22,144,128]{3,2,1,0:T(8,128)S(1)} %get-tuple-element.7.flux, f32[22,144,128]{2,1,0:T(8,128)S(1)} %get-tuple-element.8.wide), custom_call_target="tpu_custom_call" | custom-call | tf_op jit(solution)/shard_map/relax/pallas_call | solution.py:495
